TPU v7x, 32 devices: a whole 2x2x4 slice. The times are simulated.
32 devices in a mesh: groups: 2 (over y), shot: 4 (over x, core), slab: 4 (over z).
Axes of the slice: x: 2, y: 2, z: 4, core: 2. Of those that a mesh axis runs over, the one named last changes fastest.
Arguments:
- slowness: float32 [32, 192, 128], P(('groups', 'slab')), parts along dimension 0, may hold values from 0.8 to 1.25
- wave_prev: float32 [8, 16, 192, 128], P(('groups', 'shot'), 'slab'), parts along dimension 0, may hold values from -6 to 6
- wave_now: float32 [8, 16, 192, 128], P(('groups', 'shot'), 'slab'), parts along dimension 0, may hold values from -6 to 6
- memory: float32 [8, 3, 16, 192, 128], P(('groups', 'shot'), None, 'slab'), parts along dimension 0, may hold values from -6 to 6
- adjoint_now: float32 [8, 16, 192, 128], P(('groups', 'shot'), 'slab'), parts along dimension 0, may hold values from -6 to 6
- adjoint_prev: float32 [8, 16, 192, 128], P(('groups', 'shot'), 'slab'), parts along dimension 0, may hold values from -6 to 6
- wavelet: float32 [4], replicated, may hold values from -16 to 16
- src_cells: int32 [8, 64], P(('groups', 'shot')), parts along dimension 0, may hold values from 0 to 393215
- src_signs: int32 [8, 64], P(('groups', 'shot')), parts along dimension 0, may hold values from -1 to 1, as said below
- rec_cells: int32 [512], P('groups'), parts along dimension 0, may hold values from 0 to 393215
- observed: float32 [8, 4, 256], P(('groups', 'shot')), parts along dimension 0, may hold values from -6 to 6
Outputs:
- new_slowness: float32 [32, 192, 128], P(('groups', 'slab')), parts along dimension 0
- gradient: float32 [32, 192, 128], P(('groups', 'slab'), 'shot'), parts along dimension 0
There are 2 independent parts, one for each index of `groups`. A program takes and returns all parts, laid end to end along the dimension named above; an argument that names none is the same for every part. Nothing has to cross between parts.
Inputs may be any that keep to these rules, and one draw needn't show every extreme that they name: `src_signs`: each entry is -1 or +1.
All inputs are finite; a program needn't handle non-finite values.
Results may differ from a plain program's by a relative error of at most 0.0001.
Values sent between devices are 32-bit elements; how exact they have to be, the bound alone decides.
No kernel may reach another device: no remote copies, remote signals or barrier semaphores. Data moves between devices by JAX's collectives and lax.ppermute only.
A program may use at most 64 MiB of HBM per device.

v0:
```python
import jax
import jax.numpy as jnp
from jax import lax
from jax.sharding import PartitionSpec as P

STEPS = 4
center_coef = -2.5
near_coef = 4.0 / 3.0
far_coef = -1.0 / 12.0
courant = 0.14
relax_decay = (0.3, 0.7, 0.95)
relax_weight = (0.3, 0.2, 0.1)
update_rate = 0.05
tiny_eps = 1e-06


def padded_2(block, sides, width):
    for axis, dim in sides:
        count = lax.axis_size(axis)
        forward = [(i, i + 1) for i in range(count - 1)]
        backward = [(target, source) for source, target in forward]
        low = lax.ppermute(
            lax.slice_in_dim(block, block.shape[dim] - width, None, axis=dim), axis, forward
        )
        high = lax.ppermute(lax.slice_in_dim(block, 0, width, axis=dim), axis, backward)
        block = jnp.concatenate([low, block, high], axis=dim)
    return block


def laplace(padded):
    middle = padded[2:-2]
    flanks = jnp.pad(middle, ((0, 0), (2, 2), (2, 2)))
    depth_sum = near_coef * (padded[3:-1] + padded[1:-3]) + far_coef * (padded[4:] + padded[:-4])
    cross_sum = near_coef * (flanks[:, 3:-1, 2:-2] + flanks[:, 1:-3, 2:-2]) + far_coef * (
        flanks[:, 4:, 2:-2] + flanks[:, :-4, 2:-2]
    )
    along_sum = near_coef * (flanks[:, 2:-2, 3:-1] + flanks[:, 2:-2, 1:-3]) + far_coef * (
        flanks[:, 2:-2, 4:] + flanks[:, 2:-2, :-4]
    )
    return 3.0 * center_coef * middle + depth_sum + cross_sum + along_sum


def place_sources(cells, signs, start, count):
    local = cells - start
    inside = (local >= 0) & (local < count)
    slot = jnp.where(inside, local, count)
    return jnp.zeros((count,), jnp.float32).at[slot].add(signs.astype(jnp.float32), mode="drop")


def per_device(
    slowness,
    wave_prev,
    wave_now,
    memory,
    adjoint_now,
    adjoint_prev,
    wavelet,
    src_cells,
    src_signs,
    rec_cells,
    observed,
):
    depth, width, lanes = slowness.shape
    plane = width * lanes
    block = depth * plane
    offset = lax.axis_index("slab") * block
    decay = jnp.array(relax_decay, jnp.float32)[:, None, None, None]
    weight = jnp.array(relax_weight, jnp.float32)[:, None, None, None]
    rec_local = rec_cells - offset
    rec_inside = (rec_local >= 0) & (rec_local < block)
    rec_slot = jnp.where(rec_inside, rec_local, block)
    rec_safe = jnp.minimum(rec_slot, block - 1)
    scaled = courant / (slowness * slowness)
    older, current, relax = (wave_prev[0], wave_now[0], memory[0])
    saved = []
    misfits = []

    def record(field, level):
        picked = field.reshape(-1)[rec_safe]
        misfits.append(jnp.where(rec_inside, picked - observed[0, level], 0.0))

    src_field = place_sources(src_cells[0], src_signs[0], offset, block).reshape(
        depth, width, lanes
    )
    for level in range(STEPS):
        padded = padded_2(current, (("slab", 0),), 2)
        curved = laplace(padded)
        accel = curved + jnp.sum(relax, 0)
        newer = 2.0 * current - older + scaled * accel + wavelet[level] * src_field
        relax = decay * relax - weight * curved[None]
        older, current = (current, newer)
        saved.append(accel)
        record(current, level)
    back_prev, back_now = (adjoint_prev[0], adjoint_now[0])
    back_relax = jnp.zeros_like(relax)
    accum = jnp.zeros_like(slowness)
    for level in reversed(range(STEPS)):
        inject = (
            jnp.zeros((block,), jnp.float32)
            .at[rec_slot]
            .add(misfits[level], mode="drop")
            .reshape(depth, width, lanes)
        )
        united = back_now + inject
        pushed = scaled * united
        drive = pushed - jnp.sum(weight * back_relax, 0)
        padded = padded_2(drive, (("slab", 0),), 2)
        accum = accum + united * saved[level]
        back_prev, back_now = (-united, back_prev + 2.0 * united + laplace(padded))
        back_relax = decay * back_relax + pushed[None]
    local_grad = accum * (-2.0 * courant / (slowness * slowness * slowness))
    cells_all = lax.axis_size("slab") * block
    share = width // lax.axis_size("shot")
    first = lax.axis_index("shot") * share
    summed = lax.psum(local_grad, "shot")
    squares = lax.psum(jnp.sum(summed * summed), "slab")
    rms_value = jnp.sqrt(squares / cells_all + tiny_eps)
    normed = summed / rms_value
    new_slowness = slowness - update_rate * normed
    gradient = lax.dynamic_slice_in_dim(normed, first, share, 1)
    return (new_slowness, gradient)


def solution(mesh):
    in_specs = (
        P(("groups", "slab"), None, None),
        P(("groups", "shot"), "slab", None, None),
        P(("groups", "shot"), "slab", None, None),
        P(("groups", "shot"), None, "slab", None, None),
        P(("groups", "shot"), "slab", None, None),
        P(("groups", "shot"), "slab", None, None),
        P(),
        P(("groups", "shot"), None),
        P(("groups", "shot"), None),
        P("groups"),
        P(("groups", "shot"), None, None),
    )
    out_specs = (P(("groups", "slab"), None, None), P(("groups", "slab"), "shot", None))
    return jax.shard_map(
        per_device, mesh=mesh, in_specs=in_specs, out_specs=out_specs, check_vma=False
    )
```

profile of v0, /device:TPU:0, one launch (start us, length us, event | category | flops | bytes accessed | tf_op | source)
XLA Modules:
  0.0 167.0 jit_solution(11458838551574252018)
XLA Ops:
  7.2 1.1 slice_bitcast_fusion.1
  8.3 1.3 collective-permute-start
  9.6 5.6 %collective-permute-start.1 = (f32[2,192,128]{2,1,0:T(8,128)S(1)}, f32[2,192,128]{2,1,0:T(8,128)S(1)}, u32[]{:S(2)}, u32[]{:S(2)}) collective-permute-start(f32[2,192,128]{2,1,0:T(8,128)S(1)} %get-tuple-element.43), channel_id=1, source_target_pairs={{0,1},{1,2},{2,3},{4,5},{5,6},{6,7},{8,9},{9,10},{10,11},{12,13},{... | collective-permute-start | bytes 589832 | tf_op jit(solution)/shard_map/ppermute | solution.py:22
  15.2 0.7 convert_bitcast_fusion
  15.8 1.5 fusion.182
  17.3 0.7 fusion.166
  17.9 1.4 reduce_sum.74
  19.4 1.0 scatter_custom_fusion
  20.4 2.6 %broadcast_multiply_fusion.1 = (f32[98304]{0:T(1024)S(1)}, f32[98304]{0:T(1024)S(1)}, f32[98304]{0:T(1024)S(1)}, f32[98304]{0:T(1024)S(1)}) fusion(f32[98304]{0:T(1024)S(1)} %scatter_custom_fusion, f32[]{:T(128)} %bitcast.13, f32[]{:T(128)} %bitcast.15, f32[]{:T(128)} %bitcast.11, f32[]{:T(128)} %bitcast.5), kind=kLoop, calls=%fused_computation.281 | loop fusion | flops 393216 | bytes 1966096 | tf_op jit(solution)/shard_map/mul | solution.py:89
  23.2 1.3 fusion.155
  24.5 1.3 collective-permute-start.2
  25.8 4.6 %collective-permute-start.3 = (f32[2,192,128]{2,1,0:T(8,128)S(1)}, f32[2,192,128]{2,1,0:T(8,128)S(1)}, u32[]{:S(2)}, u32[]{:S(2)}) collective-permute-start(f32[2,192,128]{2,1,0:T(8,128)S(1)} %get-tuple-element.41), channel_id=1, source_target_pairs={{0,1},{1,2},{2,3},{4,5},{5,6},{6,7},{8,9},{9,10},{10,11},{12,13},{... | collective-permute-start | bytes 589832 | tf_op jit(solution)/shard_map/ppermute | solution.py:22
  30.4 0.2 fusion.2
  30.6 2.1 %collective-permute-done.2 = f32[2,192,128]{2,1,0:T(8,128)S(1)} collective-permute-done((f32[2,192,128]{2,1,0:T(8,128)S(1)}, f32[2,192,128]{2,1,0:T(8,128)S(1)}, u32[]{:S(2)}, u32[]{:S(2)}) %collective-permute-start.2) | collective-permute-done | bytes 196640 | tf_op jit(solution)/shard_map/ppermute | solution.py:25
  32.7 1.2 collective-permute-done.3
  33.9 0.5 add_add_fusion.2
  34.5 1.3 collective-permute-start.4
  35.8 5.0 %collective-permute-start.5 = (f32[2,192,128]{2,1,0:T(8,128)S(1)}, f32[2,192,128]{2,1,0:T(8,128)S(1)}, u32[]{:S(2)}, u32[]{:S(2)}) collective-permute-start(f32[2,192,128]{2,1,0:T(8,128)S(1)} %get-tuple-element.35), channel_id=1, source_target_pairs={{0,1},{1,2},{2,3},{4,5},{5,6},{6,7},{8,9},{9,10},{10,11},{12,13},{... | collective-permute-start | bytes 589832 | tf_op jit(solution)/shard_map/ppermute | solution.py:22
  40.8 0.6 fusion.181
  41.4 1.1 collective-permute-done.4
  42.5 1.5 collective-permute-done.5
  44.0 0.5 fusion.52
  44.5 0.5 fusion.1
  45.0 0.2 add_add_fusion.1
  45.2 0.8 fusion.178
  45.9 1.3 collective-permute-start.6
  47.2 5.0 %collective-permute-start.7 = (f32[2,192,128]{2,1,0:T(8,128)}, f32[2,192,128]{2,1,0:T(8,128)S(1)}, u32[]{:S(2)}, u32[]{:S(2)}) collective-permute-start(f32[2,192,128]{2,1,0:T(8,128)} %get-tuple-element.33), channel_id=1, source_target_pairs={{0,1},{1,2},{2,3},{4,5},{5,6},{6,7},{8,9},{9,10},{10,11},{12,13},{... | collective-permute-start | bytes 589832 | tf_op jit(solution)/shard_map/ppermute | solution.py:22
  52.3 0.6 compare_select_fusion.1
  52.8 2.3 %gather_fusion.3 = f32[256]{0:T(256)} fusion(f32[98304]{0:T(1024)S(1)} %bitcast.58, s32[1024]{0:T(1024)S(1)} %pad_clamp_fusion), kind=kCustom, calls=%fused_computation.3 | custom fusion | bytes 3072 | tf_op jit(solution)/shard_map/gather | solution.py:79
  55.2 2.3 %gather_fusion.2 = f32[256]{0:T(256)} fusion(f32[98304]{0:T(1024)S(1)} %bitcast.57, s32[1024]{0:T(1024)S(1)} %pad_clamp_fusion), kind=kCustom, calls=%fused_computation.2 | custom fusion | bytes 3072 | tf_op jit(solution)/shard_map/gather | solution.py:79
  57.5 2.3 %gather_fusion.1 = f32[256]{0:T(256)} fusion(f32[98304]{0:T(1024)S(1)} %bitcast.59, s32[1024]{0:T(1024)S(1)} %pad_clamp_fusion), kind=kCustom, calls=%fused_computation.1 | custom fusion | bytes 3072 | tf_op jit(solution)/shard_map/gather | solution.py:79
  59.8 0.7 copy-done.6
  60.5 1.6 add_add_fusion
  62.2 1.7 %gather_fusion = f32[256]{0:T(256)S(1)} fusion(f32[98304]{0:T(1024)S(1)} %bitcast.61, s32[1024]{0:T(1024)S(1)} %pad_clamp_fusion), kind=kCustom, calls=%fused_computation | custom fusion | bytes 3072 | tf_op jit(solution)/shard_map/gather | solution.py:79
  63.9 1.3 subtract_select_fusion.1
  65.2 2.2 %scatter_custom_fusion.1 = f32[98304]{0:T(1024)S(1)} fusion(s32[256]{0:T(256)} %compare_select_fusion.1, f32[256]{0:T(256)S(1)} %get-tuple-element.51, f32[]{:T(128)} %constant.19.clone.1), kind=kCustom, calls=%fused_computation.292 | custom fusion | flops 256 | bytes 393728 | tf_op jit(solution)/shard_map/scatter-add | solution.py:101
  67.4 0.1 fusion.168
  67.5 0.8 fusion.177
  68.3 1.3 collective-permute-start.8
  69.6 4.6 %collective-permute-start.9 = (f32[2,192,128]{2,1,0:T(8,128)}, f32[2,192,128]{2,1,0:T(8,128)S(1)}, u32[]{:S(2)}, u32[]{:S(2)}) collective-permute-start(f32[2,192,128]{2,1,0:T(8,128)} %get-tuple-element.31), channel_id=1, source_target_pairs={{0,1},{1,2},{2,3},{4,5},{5,6},{6,7},{8,9},{9,10},{10,11},{12,13},{... | collective-permute-start | bytes 589832 | tf_op jit(solution)/shard_map/ppermute | solution.py:22
  74.1 2.2 %scatter_custom_fusion.2 = f32[98304]{0:T(1024)S(1)} fusion(s32[256]{0:T(256)} %compare_select_fusion.1, f32[256]{0:T(256)} %get-tuple-element.50, f32[]{:T(128)} %constant.19.clone.1), kind=kCustom, calls=%fused_computation.290 | custom fusion | flops 256 | bytes 393728 | tf_op jit(solution)/shard_map/scatter-add | solution.py:101
  76.3 1.3 collective-permute-done.9
  77.6 0.7 copy-done.11
  78.3 1.6 fusion.167
  79.9 1.1 multiply_reduce_fusion.1
  81.0 0.1 fusion.169
  81.1 1.3 collective-permute-start.10
  82.4 4.9 %collective-permute-start.11 = (f32[2,192,128]{2,1,0:T(8,128)S(1)}, f32[2,192,128]{2,1,0:T(8,128)S(1)}, u32[]{:S(2)}, u32[]{:S(2)}) collective-permute-start(f32[2,192,128]{2,1,0:T(8,128)S(1)} %get-tuple-element.29), channel_id=1, source_target_pairs={{0,1},{1,2},{2,3},{4,5},{5,6},{6,7},{8,9},{9,10},{10,11},{12,13},{... | collective-permute-start | bytes 589832 | tf_op jit(solution)/shard_map/ppermute | solution.py:22
  87.3 2.8 %scatter_custom_fusion.3 = f32[98304]{0:T(1024)} fusion(s32[256]{0:T(256)} %compare_select_fusion.1, f32[256]{0:T(256)} %get-tuple-element.48, f32[]{:T(128)} %constant.19.clone.1), kind=kCustom, calls=%fused_computation.288 | custom fusion | flops 256 | bytes 393728 | tf_op jit(solution)/shard_map/scatter-add | solution.py:101
  90.2 0.3 collective-permute-done.11
  90.5 0.4 copy-done.8
  90.9 0.3 copy-done.10
  91.2 1.8 %multiply_subtract_fusion.2 = (f32[4,192,128]{2,1,0:T(8,128)S(1)}, f32[4,192,128]{2,1,0:T(8,128)S(1)}) fusion(f32[4,192,128]{2,1,0:T(8,128)} %get-tuple-element.5, f32[4,192,128]{2,1,0:T(8,128)S(1)} %copy-done, f32[4,192,128]{2,1,0:T(8,128)} %bitcast.66, f32[4,192,128]{2,1,0:T(8,128)S(1)} %fusion.169, f32[2,192,128]{2,1,0:T(8,128)} %copy-done.10, ...), kind=kLoop, calls=%fused_computation.275 | loop fusion | flops 3145728 | bytes 3538944 | tf_op jit(solution)/shard_map/sub | solution.py:106
  93.0 0.8 fusion.175
  93.8 1.3 collective-permute-start.12
  95.1 5.7 %collective-permute-start.13 = (f32[2,192,128]{2,1,0:T(8,128)}, f32[2,192,128]{2,1,0:T(8,128)}, u32[]{:S(2)}, u32[]{:S(2)}) collective-permute-start(f32[2,192,128]{2,1,0:T(8,128)} %get-tuple-element.27), channel_id=1, source_target_pairs={{0,1},{1,2},{2,3},{4,5},{5,6},{6,7},{8,9},{9,10},{10,11},{12,13},{... | collective-permute-start | bytes 589832 | tf_op jit(solution)/shard_map/ppermute | solution.py:22
  100.8 2.2 %scatter_custom_fusion.4 = f32[98304]{0:T(1024)S(1)} fusion(s32[256]{0:T(256)} %compare_select_fusion.1, f32[256]{0:T(256)S(1)} %get-tuple-element.49, f32[]{:T(128)} %constant.19.clone.1), kind=kCustom, calls=%fused_computation.286 | custom fusion | flops 256 | bytes 393728 | tf_op jit(solution)/shard_map/scatter-add | solution.py:101
  103.0 0.6 collective-permute-done.13
  103.6 2.6 %fusion.4 = f32[4,192,128]{2,1,0:T(8,128)} fusion(f32[4,192,128]{2,1,0:T(8,128)S(1)} %copy-done, f32[4,192,128]{2,1,0:T(8,128)} %get-tuple-element.24, f32[4,192,128]{2,1,0:T(8,128)S(1)} %bitcast.65, f32[2,192,128]{2,1,0:T(8,128)} %collective-permute-done.13, f32[4,192,128]{2,1,0:T(8,128)S(1)} %get-tuple-element.8, ...), kind=kLoop, calls=%fused_computation.104 | loop fusion | flops 3833856 | bytes 4718592 | tf_op jit(solution)/shard_map/mul | solution.py:111
  106.2 36.8 %all-reduce.9.cloned.1.call-done = f32[4,192,128]{2,1,0:T(8,128)} async-done(((f32[4,192,128]{2,1,0:T(8,128)}), f32[4,192,128]{2,1,0:T(8,128)}) %all-reduce.9.cloned.1.call-update) | async-done | bytes 393232 | tf_op jit(solution)/shard_map/psum | solution.py:115
  143.0 1.7 %multiply_reduce_fusion.2 = f32[]{:T(128)} fusion(f32[4,192,128]{2,1,0:T(8,128)} %all-reduce.9.cloned.1.call-done), kind=kLoop, calls=%fused_computation.274 | loop fusion | flops 196607 | bytes 393220 | tf_op jit(solution)/shard_map/reduce_sum | solution.py:116
  144.7 12.3 %psum.15 = f32[]{:T(128)} all-reduce(f32[]{:T(128)} %multiply_reduce_fusion.2), channel_id=1, replica_groups=mesh['groups'=2,'shot'=4,'slab'=4] {'slab'}, use_global_device_ids=true, to_apply=%region_14.15 | all-reduce | flops 1 | bytes 8 | tf_op jit(solution)/shard_map/psum | solution.py:116
  157.7 1.8 %multiply_subtract_fusion.1 = (f32[4,192,128]{2,1,0:T(8,128)}, f32[4,192,128]{2,1,0:T(8,128)S(1)}) fusion(f32[4,192,128]{2,1,0:T(8,128)S(1)} %copy-done, f32[4,192,128]{2,1,0:T(8,128)} %all-reduce.9.cloned.1.call-done, f32[]{:T(128)S(6)} %sqrt.3), kind=kLoop, calls=%fused_computation.273 | loop fusion | flops 294912 | bytes 1572868 | tf_op jit(solution)/shard_map/sub | solution.py:119
  159.5 0.6 constant_dynamic-slice_fusion
  (44 shorter events, 0.3 us)
Async XLA Ops:
  7.2 135.9 %all-reduce.9.cloned.1.call-start = ((), (), s32[]{:S(2)}) async-start(), calls=%async_computation | async-start | bytes 786432 | tf_op jit(solution)/shard_map/psum | solution.py:115
  8.3 14.8 %collective-permute-start = (f32[2,192,128]{2,1,0:T(8,128)S(1)}, f32[2,192,128]{2,1,0:T(8,128)S(1)}, u32[]{:S(2)}, u32[]{:S(2)}) collective-permute-start(f32[2,192,128]{2,1,0:T(8,128)S(1)} %get-tuple-element.42), channel_id=1, source_target_pairs={{1,0},{2,1},{3,2},{5,4},{6,5},{7,6},{9,8},{10,9},{11,10},{13,12},{... | collective-permute-start | bytes 589832 | tf_op jit(solution)/shard_map/ppermute | solution.py:25
  9.6 13.5 %collective-permute-start.1 = (f32[2,192,128]{2,1,0:T(8,128)S(1)}, f32[2,192,128]{2,1,0:T(8,128)S(1)}, u32[]{:S(2)}, u32[]{:S(2)}) collective-permute-start(f32[2,192,128]{2,1,0:T(8,128)S(1)} %get-tuple-element.43), channel_id=1, source_target_pairs={{0,1},{1,2},{2,3},{4,5},{5,6},{6,7},{8,9},{9,10},{10,11},{12,13},{... | collective-permute-start | bytes 589832 | tf_op jit(solution)/shard_map/ppermute | solution.py:22
  19.3 3.7 %copy-start.14 = (s32[256]{0:T(256)S(1)}, s32[256]{0:T(256)}, u32[]{:S(2)}) copy-start(s32[256]{0:T(256)} %param.22) | copy-start | bytes 3076
  19.3 3.8 %copy-start = (f32[4,192,128]{2,1,0:T(8,128)S(1)}, f32[4,192,128]{2,1,0:T(8,128)}, u32[]{:S(2)}) copy-start(f32[4,192,128]{2,1,0:T(8,128)} %param.13) | copy-start | bytes 1179652
  19.4 3.8 %copy-start.2 = (f32[1,4,192,128]{3,2,1,0:T(8,128)S(1)}, f32[1,4,192,128]{3,2,1,0:T(8,128)}, u32[]{:S(2)}) copy-start(f32[1,4,192,128]{3,2,1,0:T(8,128)} %param.15) | copy-start | bytes 1179652
  19.4 3.8 %copy-start.5 = (f32[1,4,192,128]{3,2,1,0:T(8,128)S(1)}, f32[1,4,192,128]{3,2,1,0:T(8,128)}, u32[]{:S(2)}) copy-start(f32[1,4,192,128]{3,2,1,0:T(8,128)} %param.14) | copy-start | bytes 1179652
  23.1 7.2 %copy-start.1 = (f32[1,3,4,192,128]{4,3,2,1,0:T(8,128)S(1)}, f32[1,3,4,192,128]{4,3,2,1,0:T(8,128)}, u32[]{:S(2)}) copy-start(f32[1,3,4,192,128]{4,3,2,1,0:T(8,128)} %param.16) | copy-start | bytes 3538948
  23.1 7.2 %copy-start.12 = (f32[3]{0:T(128)S(1)}, f32[3]{0:T(128)}, u32[]{:S(2)}) copy-start(f32[3]{0:T(128)} %constant.18.clone) | copy-start | bytes 40
  23.2 7.2 %copy-start.13 = (f32[3]{0:T(128)S(1)}, f32[3]{0:T(128)}, u32[]{:S(2)}) copy-start(f32[3]{0:T(128)} %constant.50.clone) | copy-start | bytes 40
  24.5 8.3 %collective-permute-start.2 = (f32[2,192,128]{2,1,0:T(8,128)S(1)}, f32[2,192,128]{2,1,0:T(8,128)S(1)}, u32[]{:S(2)}, u32[]{:S(2)}) collective-permute-start(f32[2,192,128]{2,1,0:T(8,128)S(1)} %get-tuple-element.40), channel_id=1, source_target_pairs={{1,0},{2,1},{3,2},{5,4},{6,5},{7,6},{9,8},{10,9},{11,10},{13,12},{... | collective-permute-start | bytes 589832 | tf_op jit(solution)/shard_map/ppermute | solution.py:25
  25.8 8.1 %collective-permute-start.3 = (f32[2,192,128]{2,1,0:T(8,128)S(1)}, f32[2,192,128]{2,1,0:T(8,128)S(1)}, u32[]{:S(2)}, u32[]{:S(2)}) collective-permute-start(f32[2,192,128]{2,1,0:T(8,128)S(1)} %get-tuple-element.41), channel_id=1, source_target_pairs={{0,1},{1,2},{2,3},{4,5},{5,6},{6,7},{8,9},{9,10},{10,11},{12,13},{... | collective-permute-start | bytes 589832 | tf_op jit(solution)/shard_map/ppermute | solution.py:22
  33.9 6.9 %copy-start.16 = (f32[1,4,256]{2,1,0:T(4,128)S(1)}, f32[1,4,256]{2,1,0:T(4,128)}, u32[]{:S(2)}) copy-start(f32[1,4,256]{2,1,0:T(4,128)} %param.23) | copy-start | bytes 12292
  34.5 8.0 %collective-permute-start.4 = (f32[2,192,128]{2,1,0:T(8,128)S(1)}, f32[2,192,128]{2,1,0:T(8,128)S(1)}, u32[]{:S(2)}, u32[]{:S(2)}) collective-permute-start(f32[2,192,128]{2,1,0:T(8,128)S(1)} %get-tuple-element.34), channel_id=1, source_target_pairs={{1,0},{2,1},{3,2},{5,4},{6,5},{7,6},{9,8},{10,9},{11,10},{13,12},{... | collective-permute-start | bytes 589832 | tf_op jit(solution)/shard_map/ppermute | solution.py:25
  35.8 8.2 %collective-permute-start.5 = (f32[2,192,128]{2,1,0:T(8,128)S(1)}, f32[2,192,128]{2,1,0:T(8,128)S(1)}, u32[]{:S(2)}, u32[]{:S(2)}) collective-permute-start(f32[2,192,128]{2,1,0:T(8,128)S(1)} %get-tuple-element.35), channel_id=1, source_target_pairs={{0,1},{1,2},{2,3},{4,5},{5,6},{6,7},{8,9},{9,10},{10,11},{12,13},{... | collective-permute-start | bytes 589832 | tf_op jit(solution)/shard_map/ppermute | solution.py:22
  45.0 7.3 %copy-start.15 = (s32[256]{0:T(256)S(1)}, s32[256]{0:T(256)}, u32[]{:S(2)}) copy-start(s32[256]{0:T(256)} %param.22) | copy-start | bytes 3076
  45.9 13.8 %collective-permute-start.6 = (f32[2,192,128]{2,1,0:T(8,128)}, f32[2,192,128]{2,1,0:T(8,128)S(1)}, u32[]{:S(2)}, u32[]{:S(2)}) collective-permute-start(f32[2,192,128]{2,1,0:T(8,128)} %get-tuple-element.32), channel_id=1, source_target_pairs={{1,0},{2,1},{3,2},{5,4},{6,5},{7,6},{9,8},{10,9},{11,10},{13,12},{... | collective-permute-start | bytes 589832 | tf_op jit(solution)/shard_map/ppermute | solution.py:25
  47.2 12.5 %collective-permute-start.7 = (f32[2,192,128]{2,1,0:T(8,128)}, f32[2,192,128]{2,1,0:T(8,128)S(1)}, u32[]{:S(2)}, u32[]{:S(2)}) collective-permute-start(f32[2,192,128]{2,1,0:T(8,128)} %get-tuple-element.33), channel_id=1, source_target_pairs={{0,1},{1,2},{2,3},{4,5},{5,6},{6,7},{8,9},{9,10},{10,11},{12,13},{... | collective-permute-start | bytes 589832 | tf_op jit(solution)/shard_map/ppermute | solution.py:22
  59.8 0.7 copy-start.6
  59.8 0.7 copy-start.7
  62.2 5.2 %copy-start.4 = (f32[1,4,192,128]{3,2,1,0:T(8,128)S(1)}, f32[1,4,192,128]{3,2,1,0:T(8,128)}, u32[]{:S(2)}) copy-start(f32[1,4,192,128]{3,2,1,0:T(8,128)} %param.17) | copy-start | bytes 1179652
  67.4 10.9 %copy-start.3 = (f32[1,4,192,128]{3,2,1,0:T(8,128)S(1)}, f32[1,4,192,128]{3,2,1,0:T(8,128)}, u32[]{:S(2)}) copy-start(f32[1,4,192,128]{3,2,1,0:T(8,128)} %param.18) | copy-start | bytes 1179652
  68.3 8.1 %collective-permute-start.8 = (f32[2,192,128]{2,1,0:T(8,128)}, f32[2,192,128]{2,1,0:T(8,128)S(1)}, u32[]{:S(2)}, u32[]{:S(2)}) collective-permute-start(f32[2,192,128]{2,1,0:T(8,128)} %get-tuple-element.30), channel_id=1, source_target_pairs={{1,0},{2,1},{3,2},{5,4},{6,5},{7,6},{9,8},{10,9},{11,10},{13,12},{... | collective-permute-start | bytes 589832 | tf_op jit(solution)/shard_map/ppermute | solution.py:25
  69.6 8.0 %collective-permute-start.9 = (f32[2,192,128]{2,1,0:T(8,128)}, f32[2,192,128]{2,1,0:T(8,128)S(1)}, u32[]{:S(2)}, u32[]{:S(2)}) collective-permute-start(f32[2,192,128]{2,1,0:T(8,128)} %get-tuple-element.31), channel_id=1, source_target_pairs={{0,1},{1,2},{2,3},{4,5},{5,6},{6,7},{8,9},{9,10},{10,11},{12,13},{... | collective-permute-start | bytes 589832 | tf_op jit(solution)/shard_map/ppermute | solution.py:22
  76.3 1.3 copy-start.9
  77.6 0.7 copy-start.11
  81.1 9.1 %collective-permute-start.10 = (f32[2,192,128]{2,1,0:T(8,128)S(1)}, f32[2,192,128]{2,1,0:T(8,128)S(1)}, u32[]{:S(2)}, u32[]{:S(2)}) collective-permute-start(f32[2,192,128]{2,1,0:T(8,128)S(1)} %get-tuple-element.28), channel_id=1, source_target_pairs={{1,0},{2,1},{3,2},{5,4},{6,5},{7,6},{9,8},{10,9},{11,10},{13,12},{... | collective-permute-start | bytes 589832 | tf_op jit(solution)/shard_map/ppermute | solution.py:25
  82.4 8.1 %collective-permute-start.11 = (f32[2,192,128]{2,1,0:T(8,128)S(1)}, f32[2,192,128]{2,1,0:T(8,128)S(1)}, u32[]{:S(2)}, u32[]{:S(2)}) collective-permute-start(f32[2,192,128]{2,1,0:T(8,128)S(1)} %get-tuple-element.29), channel_id=1, source_target_pairs={{0,1},{1,2},{2,3},{4,5},{5,6},{6,7},{8,9},{9,10},{10,11},{12,13},{... | collective-permute-start | bytes 589832 | tf_op jit(solution)/shard_map/ppermute | solution.py:22
  90.2 0.7 copy-start.8
  90.5 0.7 copy-start.10
  93.8 9.2 %collective-permute-start.12 = (f32[2,192,128]{2,1,0:T(8,128)}, f32[2,192,128]{2,1,0:T(8,128)}, u32[]{:S(2)}, u32[]{:S(2)}) collective-permute-start(f32[2,192,128]{2,1,0:T(8,128)} %get-tuple-element.26), channel_id=1, source_target_pairs={{1,0},{2,1},{3,2},{5,4},{6,5},{7,6},{9,8},{10,9},{11,10},{13,12},{... | collective-permute-start | bytes 589832 | tf_op jit(solution)/shard_map/ppermute | solution.py:25
  95.1 8.5 %collective-permute-start.13 = (f32[2,192,128]{2,1,0:T(8,128)}, f32[2,192,128]{2,1,0:T(8,128)}, u32[]{:S(2)}, u32[]{:S(2)}) collective-permute-start(f32[2,192,128]{2,1,0:T(8,128)} %get-tuple-element.27), channel_id=1, source_target_pairs={{0,1},{1,2},{2,3},{4,5},{5,6},{6,7},{8,9},{9,10},{10,11},{12,13},{... | collective-permute-start | bytes 589832 | tf_op jit(solution)/shard_map/ppermute | solution.py:22
Sparse Core Ops, SparseCore 0:
  106.3 36.6 all-reduce.8
where the time goes:
time: 168 us; the launch traced here: 167 us
  waiting for transfers between devices  44.9 us (27%)
  starting transfers between devices  44.4 us (26%)
  other arithmetic  33.3 us (20%)
  local copies, waits for them, and re-layouts  17 us (10%)
  between operations  15.2 us (9%)
  blocking collectives  12.3 us (7%)
    psum x1, waiting for transfers between devices, per_device(): summed = lax.psum(local_grad, 'shot')  36.8 us
    ppermute x7, starting transfers between devices, padded_2(): lax.ppermute(lax.slice_in_dim(block, block.shape[dim] - width, None, axis...  35.4 us
    psum x1, blocking collectives, per_device(): squares = lax.psum(jnp.sum(summed * summed), 'slab')  12.3 us
    scatter-add x4, other arithmetic, per_device(): inject = jnp.zeros((block,), jnp.float32).at[rec_slot].add(misfits[level]...  9.37 us
    ppermute x7, starting transfers between devices, padded_2(): lax.ppermute(lax.slice_in_dim(block, 0, width, axis=dim), axis, backward)  9.01 us
    gather x4, local copies, waits for them, and re-layouts, record(): picked = field.reshape(-1)[rec_safe]  8.65 us
    ppermute x7, waiting for transfers between devices, padded_2(): lax.ppermute(lax.slice_in_dim(block, block.shape[dim] - width, None, axis...  4.85 us
    add x4, other arithmetic, per_device(): newer = 2.0 * current - older + scaled * accel + wavelet[level] * src_field  3.63 us
  transfers between devices with their start and end apart: 15, of which 8 were waited for; matrix products, arithmetic and copies ran while one was open for 14% of the time, Pallas kernels for 0%

commit v1 on v0

--- a/solution.py
+++ b/solution.py
@@ -112,7 +112,15 @@
     cells_all = lax.axis_size("slab") * block
     share = width // lax.axis_size("shot")
     first = lax.axis_index("shot") * share
-    summed = lax.psum(local_grad, "shot")
+    size_here = jax.lax.axis_size("shot")
+    summed, carry = (local_grad, 0)
+    while 1 << carry < size_here:
+        table = []
+        for idx in range(size_here):
+            table.append((idx, idx ^ 1 << carry))
+        y2 = jax.lax.ppermute(summed, axis_name="shot", perm=table)
+        summed = summed + y2
+        carry = carry + 1
     squares = lax.psum(jnp.sum(summed * summed), "slab")
     rms_value = jnp.sqrt(squares / cells_all + tiny_eps)
     normed = summed / rms_value

time: 168 us -> 131 us (0.78)
  waiting for transfers between devices: 44.9 us -> 19.3 us
  between operations: 15.2 us -> 1.79 us
  other arithmetic: 33.3 us -> 30.5 us
  blocking collectives: 12.3 us -> 15 us
  starting transfers between devices: 44.4 us -> 46.2 us
    psum x1 -> x0, waiting for transfers between devices: 36.8 us -> none  [per_device(): summed = lax.psum(local_grad, 'shot')]
    ppermute x0 -> x2, waiting for transfers between devices: none -> 11.2 us  [per_device(): y2 = jax.lax.ppermute(summed, axis_name='shot', perm=table)]
    psum x1, blocking collectives: 12.3 us -> 15 us  [per_device(): squares = lax.psum(jnp.sum(summed * summed), 'slab')]
    ppermute x0 -> x2, starting transfers between devices: none -> 1.78 us  [per_device(): y2 = jax.lax.ppermute(summed, axis_name='shot', perm=table)]
  transfers between devices with their start and end apart: 15 -> 16, of which waited for: 8 -> 9; matrix products, arithmetic and copies ran while one was open for 14% -> 18% of each run, Pallas kernels for 0% -> 0%
where the time goes in v1:
time: 131 us; the launch traced here: 130 us
  starting transfers between devices  46.2 us (35%)
  other arithmetic  30.5 us (23%)
  waiting for transfers between devices  19.3 us (15%)
  local copies, waits for them, and re-layouts  17 us (13%)
  blocking collectives  15 us (11%)
  between operations  1.79 us (1%)
    ppermute x7, starting transfers between devices, padded_2(): lax.ppermute(lax.slice_in_dim(block, block.shape[dim] - width, None, axis...  35.4 us
    psum x1, blocking collectives, per_device(): squares = lax.psum(jnp.sum(summed * summed), 'slab')  15 us
    ppermute x2, waiting for transfers between devices, per_device(): y2 = jax.lax.ppermute(summed, axis_name='shot', perm=table)  11.2 us
    scatter-add x4, other arithmetic, per_device(): inject = jnp.zeros((block,), jnp.float32).at[rec_slot].add(misfits[level]...  9.35 us
    ppermute x7, starting transfers between devices, padded_2(): lax.ppermute(lax.slice_in_dim(block, 0, width, axis=dim), axis, backward)  9.01 us
    gather x4, local copies, waits for them, and re-layouts, record(): picked = field.reshape(-1)[rec_safe]  8.69 us
    ppermute x7, waiting for transfers between devices, padded_2(): lax.ppermute(lax.slice_in_dim(block, block.shape[dim] - width, None, axis...  4.87 us
    add x4, other arithmetic, per_device(): newer = 2.0 * current - older + scaled * accel + wavelet[level] * src_field  3.63 us
  transfers between devices with their start and end apart: 16, of which 9 were waited for; matrix products, arithmetic and copies ran while one was open for 18% of the time, Pallas kernels for 0%

profile of v1, /device:TPU:0, one launch (start us, length us, event | category | flops | bytes accessed | tf_op | source)
XLA Modules:
  0.0 129.8 jit_solution(16587008127004267591)
XLA Ops:
  0.6 1.1 slice_bitcast_fusion.1
  1.7 1.3 collective-permute-start
  3.0 5.6 %collective-permute-start.1 = (f32[2,192,128]{2,1,0:T(8,128)S(1)}, f32[2,192,128]{2,1,0:T(8,128)S(1)}, u32[]{:S(2)}, u32[]{:S(2)}) collective-permute-start(f32[2,192,128]{2,1,0:T(8,128)S(1)} %get-tuple-element.45), channel_id=1, source_target_pairs={{0,1},{1,2},{2,3},{4,5},{5,6},{6,7},{8,9},{9,10},{10,11},{12,13},{... | collective-permute-start | bytes 589832 | tf_op jit(solution)/shard_map/ppermute | solution.py:22
  8.6 0.7 convert_bitcast_fusion
  9.3 1.5 %fusion.182 = (f32[1]{0:T(128)}, f32[1]{0:T(128)}, f32[1]{0:T(128)}, f32[1]{0:T(128)}) fusion(f32[4]{0:T(128)} %param.19), kind=kLoop, calls=%fused_computation.320 | loop fusion | bytes 32 | tf_op jit(solution)/shard_map/slice | solution.py:89
  10.7 0.7 fusion.166
  11.4 1.4 %reduce_sum.74 = f32[4,192,128]{2,1,0:T(8,128)S(1)} reduce(f32[1,3,4,192,128]{4,3,2,1,0:T(8,128)} %param.16, f32[]{:T(128)} %constant.19.clone.1), dimensions={0,1}, to_apply=%region_0.1 | reduce | flops 196608 | bytes 1572868 | tf_op jit(solution)/shard_map/reduce_sum | solution.py:88
  12.8 1.0 scatter_custom_fusion
  13.8 2.6 %broadcast_multiply_fusion.1 = (f32[98304]{0:T(1024)S(1)}, f32[98304]{0:T(1024)S(1)}, f32[98304]{0:T(1024)S(1)}, f32[98304]{0:T(1024)S(1)}) fusion(f32[98304]{0:T(1024)S(1)} %scatter_custom_fusion, f32[]{:T(128)} %bitcast.13, f32[]{:T(128)} %bitcast.15, f32[]{:T(128)} %bitcast.11, f32[]{:T(128)} %bitcast.5), kind=kLoop, calls=%fused_computation.281 | loop fusion | flops 393216 | bytes 1966096 | tf_op jit(solution)/shard_map/mul | solution.py:89
  16.6 1.3 fusion.155
  17.9 1.3 collective-permute-start.2
  19.2 4.6 %collective-permute-start.3 = (f32[2,192,128]{2,1,0:T(8,128)S(1)}, f32[2,192,128]{2,1,0:T(8,128)S(1)}, u32[]{:S(2)}, u32[]{:S(2)}) collective-permute-start(f32[2,192,128]{2,1,0:T(8,128)S(1)} %get-tuple-element.43), channel_id=1, source_target_pairs={{0,1},{1,2},{2,3},{4,5},{5,6},{6,7},{8,9},{9,10},{10,11},{12,13},{... | collective-permute-start | bytes 589832 | tf_op jit(solution)/shard_map/ppermute | solution.py:22
  23.8 0.2 fusion.2
  24.1 2.1 %collective-permute-done.2 = f32[2,192,128]{2,1,0:T(8,128)S(1)} collective-permute-done((f32[2,192,128]{2,1,0:T(8,128)S(1)}, f32[2,192,128]{2,1,0:T(8,128)S(1)}, u32[]{:S(2)}, u32[]{:S(2)}) %collective-permute-start.2) | collective-permute-done | bytes 196640 | tf_op jit(solution)/shard_map/ppermute | solution.py:25
  26.2 1.2 collective-permute-done.3
  27.3 0.5 add_add_fusion.2
  27.9 1.3 collective-permute-start.4
  29.2 5.0 %collective-permute-start.5 = (f32[2,192,128]{2,1,0:T(8,128)S(1)}, f32[2,192,128]{2,1,0:T(8,128)S(1)}, u32[]{:S(2)}, u32[]{:S(2)}) collective-permute-start(f32[2,192,128]{2,1,0:T(8,128)S(1)} %get-tuple-element.37), channel_id=1, source_target_pairs={{0,1},{1,2},{2,3},{4,5},{5,6},{6,7},{8,9},{9,10},{10,11},{12,13},{... | collective-permute-start | bytes 589832 | tf_op jit(solution)/shard_map/ppermute | solution.py:22
  34.3 0.6 fusion.181
  34.9 1.1 collective-permute-done.4
  35.9 1.5 %collective-permute-done.5 = f32[2,192,128]{2,1,0:T(8,128)S(1)} collective-permute-done((f32[2,192,128]{2,1,0:T(8,128)S(1)}, f32[2,192,128]{2,1,0:T(8,128)S(1)}, u32[]{:S(2)}, u32[]{:S(2)}) %collective-permute-start.5) | collective-permute-done | bytes 196640 | tf_op jit(solution)/shard_map/ppermute | solution.py:22
  37.4 0.5 fusion.52
  37.9 0.5 fusion.1
  38.4 0.2 add_add_fusion.1
  38.6 0.8 fusion.178
  39.3 1.3 collective-permute-start.6
  40.6 5.0 %collective-permute-start.7 = (f32[2,192,128]{2,1,0:T(8,128)}, f32[2,192,128]{2,1,0:T(8,128)S(1)}, u32[]{:S(2)}, u32[]{:S(2)}) collective-permute-start(f32[2,192,128]{2,1,0:T(8,128)} %get-tuple-element.35), channel_id=1, source_target_pairs={{0,1},{1,2},{2,3},{4,5},{5,6},{6,7},{8,9},{9,10},{10,11},{12,13},{... | collective-permute-start | bytes 589832 | tf_op jit(solution)/shard_map/ppermute | solution.py:22
  45.7 0.6 compare_select_fusion.1
  46.2 2.3 %gather_fusion.3 = f32[256]{0:T(256)} fusion(f32[98304]{0:T(1024)S(1)} %bitcast.58, s32[1024]{0:T(1024)S(1)} %pad_clamp_fusion), kind=kCustom, calls=%fused_computation.3 | custom fusion | bytes 3072 | tf_op jit(solution)/shard_map/gather | solution.py:79
  48.6 2.3 %gather_fusion.2 = f32[256]{0:T(256)} fusion(f32[98304]{0:T(1024)S(1)} %bitcast.57, s32[1024]{0:T(1024)S(1)} %pad_clamp_fusion), kind=kCustom, calls=%fused_computation.2 | custom fusion | bytes 3072 | tf_op jit(solution)/shard_map/gather | solution.py:79
  50.9 2.3 %gather_fusion.1 = f32[256]{0:T(256)} fusion(f32[98304]{0:T(1024)S(1)} %bitcast.59, s32[1024]{0:T(1024)S(1)} %pad_clamp_fusion), kind=kCustom, calls=%fused_computation.1 | custom fusion | bytes 3072 | tf_op jit(solution)/shard_map/gather | solution.py:79
  53.2 0.7 copy-done.6
  54.0 1.6 %add_add_fusion = (f32[4,192,128]{2,1,0:T(8,128)S(1)}, f32[4,192,128]{2,1,0:T(8,128)S(1)}) fusion(f32[4,192,128]{2,1,0:T(8,128)S(1)} %bitcast.62, f32[4,192,128]{2,1,0:T(8,128)S(1)} %get-tuple-element.20, f32[4,192,128]{2,1,0:T(8,128)S(1)} %get-tuple-element.18, f32[4,192,128]{2,1,0:T(8,128)S(1)} %copy-done, f32[4,192,128]{2,1,0:T(8,128)S(1)} %get-tuple-element.3, ...), kind=kLoop, calls=%fused_computation.276 | loop fusion | flops 3047424 | bytes 3145728 | tf_op jit(solution)/shard_map/add | solution.py:89
  55.6 1.7 %gather_fusion = f32[256]{0:T(256)S(1)} fusion(f32[98304]{0:T(1024)S(1)} %bitcast.61, s32[1024]{0:T(1024)S(1)} %pad_clamp_fusion), kind=kCustom, calls=%fused_computation | custom fusion | bytes 3072 | tf_op jit(solution)/shard_map/gather | solution.py:79
  57.4 1.3 subtract_select_fusion.1
  58.6 2.2 %scatter_custom_fusion.1 = f32[98304]{0:T(1024)S(1)} fusion(s32[256]{0:T(256)} %compare_select_fusion.1, f32[256]{0:T(256)S(1)} %get-tuple-element.53, f32[]{:T(128)} %constant.19.clone.1), kind=kCustom, calls=%fused_computation.292 | custom fusion | flops 256 | bytes 393728 | tf_op jit(solution)/shard_map/scatter-add | solution.py:101
  60.9 0.8 fusion.177
  61.7 1.3 collective-permute-start.8
  63.0 4.6 %collective-permute-start.9 = (f32[2,192,128]{2,1,0:T(8,128)}, f32[2,192,128]{2,1,0:T(8,128)S(1)}, u32[]{:S(2)}, u32[]{:S(2)}) collective-permute-start(f32[2,192,128]{2,1,0:T(8,128)} %get-tuple-element.33), channel_id=1, source_target_pairs={{0,1},{1,2},{2,3},{4,5},{5,6},{6,7},{8,9},{9,10},{10,11},{12,13},{... | collective-permute-start | bytes 589832 | tf_op jit(solution)/shard_map/ppermute | solution.py:22
  67.6 2.2 %scatter_custom_fusion.2 = f32[98304]{0:T(1024)S(1)} fusion(s32[256]{0:T(256)} %compare_select_fusion.1, f32[256]{0:T(256)} %get-tuple-element.52, f32[]{:T(128)} %constant.19.clone.1), kind=kCustom, calls=%fused_computation.290 | custom fusion | flops 256 | bytes 393728 | tf_op jit(solution)/shard_map/scatter-add | solution.py:101
  69.8 1.3 collective-permute-done.9
  71.0 0.7 copy-done.11
  71.7 1.6 %fusion.167 = (f32[4,192,128]{2,1,0:T(8,128)S(1)}, f32[4,192,128]{2,1,0:T(8,128)S(1)}) fusion(f32[4,192,128]{2,1,0:T(8,128)S(1)} %copy-done, f32[4,192,128]{2,1,0:T(8,128)S(1)} %bitcast.67, f32[4,192,128]{2,1,0:T(8,128)S(1)} %get-tuple-element.14, f32[2,192,128]{2,1,0:T(8,128)} %copy-done.11, f32[2,192,128]{2,1,0:T(8,128)} %copy-done.9, ...), kind=kLoop, calls=%fused_computation.310 | loop fusion | flops 2949120 | bytes 3145728 | tf_op jit(solution)/shard_map/mul | solution.py:105
  73.3 1.1 multiply_reduce_fusion.1
  74.6 1.3 collective-permute-start.10
  75.9 4.9 %collective-permute-start.11 = (f32[2,192,128]{2,1,0:T(8,128)S(1)}, f32[2,192,128]{2,1,0:T(8,128)S(1)}, u32[]{:S(2)}, u32[]{:S(2)}) collective-permute-start(f32[2,192,128]{2,1,0:T(8,128)S(1)} %get-tuple-element.31), channel_id=1, source_target_pairs={{0,1},{1,2},{2,3},{4,5},{5,6},{6,7},{8,9},{9,10},{10,11},{12,13},{... | collective-permute-start | bytes 589832 | tf_op jit(solution)/shard_map/ppermute | solution.py:22
  80.8 2.8 %scatter_custom_fusion.3 = f32[98304]{0:T(1024)} fusion(s32[256]{0:T(256)} %compare_select_fusion.1, f32[256]{0:T(256)} %get-tuple-element.50, f32[]{:T(128)} %constant.19.clone.1), kind=kCustom, calls=%fused_computation.288 | custom fusion | flops 256 | bytes 393728 | tf_op jit(solution)/shard_map/scatter-add | solution.py:101
  83.6 0.3 collective-permute-done.11
  83.9 0.3 copy-done.8
  84.3 0.3 copy-done.10
  84.6 1.8 %multiply_subtract_fusion.2 = (f32[4,192,128]{2,1,0:T(8,128)S(1)}, f32[4,192,128]{2,1,0:T(8,128)S(1)}) fusion(f32[4,192,128]{2,1,0:T(8,128)} %get-tuple-element.5, f32[4,192,128]{2,1,0:T(8,128)S(1)} %copy-done, f32[4,192,128]{2,1,0:T(8,128)} %bitcast.66, f32[4,192,128]{2,1,0:T(8,128)S(1)} %fusion.169, f32[2,192,128]{2,1,0:T(8,128)} %copy-done.10, ...), kind=kLoop, calls=%fused_computation.275 | loop fusion | flops 3145728 | bytes 3538944 | tf_op jit(solution)/shard_map/sub | solution.py:106
  86.5 0.8 fusion.175
  87.2 1.3 collective-permute-start.12
  88.5 5.7 %collective-permute-start.13 = (f32[2,192,128]{2,1,0:T(8,128)}, f32[2,192,128]{2,1,0:T(8,128)}, u32[]{:S(2)}, u32[]{:S(2)}) collective-permute-start(f32[2,192,128]{2,1,0:T(8,128)} %get-tuple-element.29), channel_id=1, source_target_pairs={{0,1},{1,2},{2,3},{4,5},{5,6},{6,7},{8,9},{9,10},{10,11},{12,13},{... | collective-permute-start | bytes 589832 | tf_op jit(solution)/shard_map/ppermute | solution.py:22
  94.2 2.2 %scatter_custom_fusion.4 = f32[98304]{0:T(1024)S(1)} fusion(s32[256]{0:T(256)} %compare_select_fusion.1, f32[256]{0:T(256)S(1)} %get-tuple-element.51, f32[]{:T(128)} %constant.19.clone.1), kind=kCustom, calls=%fused_computation.286 | custom fusion | flops 256 | bytes 393728 | tf_op jit(solution)/shard_map/scatter-add | solution.py:101
  96.4 0.6 collective-permute-done.13
  97.0 1.9 %fusion.4 = f32[4,192,128]{2,1,0:T(8,128)S(1)} fusion(f32[4,192,128]{2,1,0:T(8,128)S(1)} %copy-done, f32[4,192,128]{2,1,0:T(8,128)} %get-tuple-element.26, f32[4,192,128]{2,1,0:T(8,128)S(1)} %bitcast.65, f32[2,192,128]{2,1,0:T(8,128)} %collective-permute-done.13, f32[4,192,128]{2,1,0:T(8,128)S(1)} %get-tuple-element.10, ...), kind=kLoop, calls=%fused_computation.104 | loop fusion | flops 3833856 | bytes 4718592 | tf_op jit(solution)/shard_map/mul | solution.py:111
  99.0 1.7 %collective-permute-done.14 = f32[4,192,128]{2,1,0:T(8,128)S(1)} collective-permute-done((f32[4,192,128]{2,1,0:T(8,128)S(1)}, f32[4,192,128]{2,1,0:T(8,128)S(1)}, u32[]{:S(2)}, u32[]{:S(2)}) %collective-permute-start.14) | collective-permute-done | bytes 393248 | tf_op jit(solution)/shard_map/ppermute | solution.py:121
  100.7 1.7 %collective-permute-start.15 = (f32[4,192,128]{2,1,0:T(8,128)S(1)}, f32[4,192,128]{2,1,0:T(8,128)S(1)}, u32[]{:S(2)}, u32[]{:S(2)}) collective-permute-start(f32[4,192,128]{2,1,0:T(8,128)S(1)} %add.519), channel_id=1, source_target_pairs={{0,8},{4,12},{8,0},{12,4},{1,9},{5,13},{9,1},{13,5},{2,10},{6,14},... | collective-permute-start | bytes 1179656 | tf_op jit(solution)/shard_map/ppermute | solution.py:121
  102.4 9.5 %collective-permute-done.15 = f32[4,192,128]{2,1,0:T(8,128)S(1)} collective-permute-done((f32[4,192,128]{2,1,0:T(8,128)S(1)}, f32[4,192,128]{2,1,0:T(8,128)S(1)}, u32[]{:S(2)}, u32[]{:S(2)}) %collective-permute-start.15) | collective-permute-done | bytes 393248 | tf_op jit(solution)/shard_map/ppermute | solution.py:121
  112.0 0.7 multiply_reduce_fusion.2
  112.7 15.0 %psum.7 = f32[]{:T(128)} all-reduce(f32[]{:T(128)} %get-tuple-element.8), channel_id=1, replica_groups=mesh['groups'=2,'shot'=4,'slab'=4] {'slab'}, use_global_device_ids=true, to_apply=%region_13.14 | all-reduce | flops 1 | bytes 8 | tf_op jit(solution)/shard_map/psum | solution.py:124
  128.4 0.8 multiply_subtract_fusion.1
  129.2 0.6 constant_dynamic-slice_fusion
  (46 shorter events, 0.5 us)
Async XLA Ops:
  1.7 14.8 %collective-permute-start = (f32[2,192,128]{2,1,0:T(8,128)S(1)}, f32[2,192,128]{2,1,0:T(8,128)S(1)}, u32[]{:S(2)}, u32[]{:S(2)}) collective-permute-start(f32[2,192,128]{2,1,0:T(8,128)S(1)} %get-tuple-element.44), channel_id=1, source_target_pairs={{1,0},{2,1},{3,2},{5,4},{6,5},{7,6},{9,8},{10,9},{11,10},{13,12},{... | collective-permute-start | bytes 589832 | tf_op jit(solution)/shard_map/ppermute | solution.py:25
  3.0 13.5 %collective-permute-start.1 = (f32[2,192,128]{2,1,0:T(8,128)S(1)}, f32[2,192,128]{2,1,0:T(8,128)S(1)}, u32[]{:S(2)}, u32[]{:S(2)}) collective-permute-start(f32[2,192,128]{2,1,0:T(8,128)S(1)} %get-tuple-element.45), channel_id=1, source_target_pairs={{0,1},{1,2},{2,3},{4,5},{5,6},{6,7},{8,9},{9,10},{10,11},{12,13},{... | collective-permute-start | bytes 589832 | tf_op jit(solution)/shard_map/ppermute | solution.py:22
  12.8 3.7 %copy-start.14 = (s32[256]{0:T(256)S(1)}, s32[256]{0:T(256)}, u32[]{:S(2)}) copy-start(s32[256]{0:T(256)} %param.22) | copy-start | bytes 3076
  12.8 3.7 %copy-start = (f32[4,192,128]{2,1,0:T(8,128)S(1)}, f32[4,192,128]{2,1,0:T(8,128)}, u32[]{:S(2)}) copy-start(f32[4,192,128]{2,1,0:T(8,128)} %param.13) | copy-start | bytes 1179652
  12.8 3.7 %copy-start.2 = (f32[1,4,192,128]{3,2,1,0:T(8,128)S(1)}, f32[1,4,192,128]{3,2,1,0:T(8,128)}, u32[]{:S(2)}) copy-start(f32[1,4,192,128]{3,2,1,0:T(8,128)} %param.15) | copy-start | bytes 1179652
  12.8 3.7 %copy-start.5 = (f32[1,4,192,128]{3,2,1,0:T(8,128)S(1)}, f32[1,4,192,128]{3,2,1,0:T(8,128)}, u32[]{:S(2)}) copy-start(f32[1,4,192,128]{3,2,1,0:T(8,128)} %param.14) | copy-start | bytes 1179652
  16.5 7.2 %copy-start.1 = (f32[1,3,4,192,128]{4,3,2,1,0:T(8,128)S(1)}, f32[1,3,4,192,128]{4,3,2,1,0:T(8,128)}, u32[]{:S(2)}) copy-start(f32[1,3,4,192,128]{4,3,2,1,0:T(8,128)} %param.16) | copy-start | bytes 3538948
  16.6 7.2 %copy-start.12 = (f32[3]{0:T(128)S(1)}, f32[3]{0:T(128)}, u32[]{:S(2)}) copy-start(f32[3]{0:T(128)} %constant.18.clone) | copy-start | bytes 40
  16.6 7.2 %copy-start.13 = (f32[3]{0:T(128)S(1)}, f32[3]{0:T(128)}, u32[]{:S(2)}) copy-start(f32[3]{0:T(128)} %constant.50.clone) | copy-start | bytes 40
  17.9 8.3 %collective-permute-start.2 = (f32[2,192,128]{2,1,0:T(8,128)S(1)}, f32[2,192,128]{2,1,0:T(8,128)S(1)}, u32[]{:S(2)}, u32[]{:S(2)}) collective-permute-start(f32[2,192,128]{2,1,0:T(8,128)S(1)} %get-tuple-element.42), channel_id=1, source_target_pairs={{1,0},{2,1},{3,2},{5,4},{6,5},{7,6},{9,8},{10,9},{11,10},{13,12},{... | collective-permute-start | bytes 589832 | tf_op jit(solution)/shard_map/ppermute | solution.py:25
  19.2 8.1 %collective-permute-start.3 = (f32[2,192,128]{2,1,0:T(8,128)S(1)}, f32[2,192,128]{2,1,0:T(8,128)S(1)}, u32[]{:S(2)}, u32[]{:S(2)}) collective-permute-start(f32[2,192,128]{2,1,0:T(8,128)S(1)} %get-tuple-element.43), channel_id=1, source_target_pairs={{0,1},{1,2},{2,3},{4,5},{5,6},{6,7},{8,9},{9,10},{10,11},{12,13},{... | collective-permute-start | bytes 589832 | tf_op jit(solution)/shard_map/ppermute | solution.py:22
  27.3 6.9 %copy-start.16 = (f32[1,4,256]{2,1,0:T(4,128)S(1)}, f32[1,4,256]{2,1,0:T(4,128)}, u32[]{:S(2)}) copy-start(f32[1,4,256]{2,1,0:T(4,128)} %param.23) | copy-start | bytes 12292
  27.9 8.0 %collective-permute-start.4 = (f32[2,192,128]{2,1,0:T(8,128)S(1)}, f32[2,192,128]{2,1,0:T(8,128)S(1)}, u32[]{:S(2)}, u32[]{:S(2)}) collective-permute-start(f32[2,192,128]{2,1,0:T(8,128)S(1)} %get-tuple-element.36), channel_id=1, source_target_pairs={{1,0},{2,1},{3,2},{5,4},{6,5},{7,6},{9,8},{10,9},{11,10},{13,12},{... | collective-permute-start | bytes 589832 | tf_op jit(solution)/shard_map/ppermute | solution.py:25
  29.2 8.2 %collective-permute-start.5 = (f32[2,192,128]{2,1,0:T(8,128)S(1)}, f32[2,192,128]{2,1,0:T(8,128)S(1)}, u32[]{:S(2)}, u32[]{:S(2)}) collective-permute-start(f32[2,192,128]{2,1,0:T(8,128)S(1)} %get-tuple-element.37), channel_id=1, source_target_pairs={{0,1},{1,2},{2,3},{4,5},{5,6},{6,7},{8,9},{9,10},{10,11},{12,13},{... | collective-permute-start | bytes 589832 | tf_op jit(solution)/shard_map/ppermute | solution.py:22
  38.4 7.3 %copy-start.15 = (s32[256]{0:T(256)S(1)}, s32[256]{0:T(256)}, u32[]{:S(2)}) copy-start(s32[256]{0:T(256)} %param.22) | copy-start | bytes 3076
  39.3 13.9 %collective-permute-start.6 = (f32[2,192,128]{2,1,0:T(8,128)}, f32[2,192,128]{2,1,0:T(8,128)S(1)}, u32[]{:S(2)}, u32[]{:S(2)}) collective-permute-start(f32[2,192,128]{2,1,0:T(8,128)} %get-tuple-element.34), channel_id=1, source_target_pairs={{1,0},{2,1},{3,2},{5,4},{6,5},{7,6},{9,8},{10,9},{11,10},{13,12},{... | collective-permute-start | bytes 589832 | tf_op jit(solution)/shard_map/ppermute | solution.py:25
  40.6 12.6 %collective-permute-start.7 = (f32[2,192,128]{2,1,0:T(8,128)}, f32[2,192,128]{2,1,0:T(8,128)S(1)}, u32[]{:S(2)}, u32[]{:S(2)}) collective-permute-start(f32[2,192,128]{2,1,0:T(8,128)} %get-tuple-element.35), channel_id=1, source_target_pairs={{0,1},{1,2},{2,3},{4,5},{5,6},{6,7},{8,9},{9,10},{10,11},{12,13},{... | collective-permute-start | bytes 589832 | tf_op jit(solution)/shard_map/ppermute | solution.py:22
  53.2 0.7 copy-start.6
  53.2 0.7 copy-start.7
  55.6 5.2 %copy-start.4 = (f32[1,4,192,128]{3,2,1,0:T(8,128)S(1)}, f32[1,4,192,128]{3,2,1,0:T(8,128)}, u32[]{:S(2)}) copy-start(f32[1,4,192,128]{3,2,1,0:T(8,128)} %param.17) | copy-start | bytes 1179652
  60.8 10.9 %copy-start.3 = (f32[1,4,192,128]{3,2,1,0:T(8,128)S(1)}, f32[1,4,192,128]{3,2,1,0:T(8,128)}, u32[]{:S(2)}) copy-start(f32[1,4,192,128]{3,2,1,0:T(8,128)} %param.18) | copy-start | bytes 1179652
  61.7 8.1 %collective-permute-start.8 = (f32[2,192,128]{2,1,0:T(8,128)}, f32[2,192,128]{2,1,0:T(8,128)S(1)}, u32[]{:S(2)}, u32[]{:S(2)}) collective-permute-start(f32[2,192,128]{2,1,0:T(8,128)} %get-tuple-element.32), channel_id=1, source_target_pairs={{1,0},{2,1},{3,2},{5,4},{6,5},{7,6},{9,8},{10,9},{11,10},{13,12},{... | collective-permute-start | bytes 589832 | tf_op jit(solution)/shard_map/ppermute | solution.py:25
  63.0 8.0 %collective-permute-start.9 = (f32[2,192,128]{2,1,0:T(8,128)}, f32[2,192,128]{2,1,0:T(8,128)S(1)}, u32[]{:S(2)}, u32[]{:S(2)}) collective-permute-start(f32[2,192,128]{2,1,0:T(8,128)} %get-tuple-element.33), channel_id=1, source_target_pairs={{0,1},{1,2},{2,3},{4,5},{5,6},{6,7},{8,9},{9,10},{10,11},{12,13},{... | collective-permute-start | bytes 589832 | tf_op jit(solution)/shard_map/ppermute | solution.py:22
  69.8 1.3 copy-start.9
  71.0 0.7 copy-start.11
  74.6 9.0 %collective-permute-start.10 = (f32[2,192,128]{2,1,0:T(8,128)S(1)}, f32[2,192,128]{2,1,0:T(8,128)S(1)}, u32[]{:S(2)}, u32[]{:S(2)}) collective-permute-start(f32[2,192,128]{2,1,0:T(8,128)S(1)} %get-tuple-element.30), channel_id=1, source_target_pairs={{1,0},{2,1},{3,2},{5,4},{6,5},{7,6},{9,8},{10,9},{11,10},{13,12},{... | collective-permute-start | bytes 589832 | tf_op jit(solution)/shard_map/ppermute | solution.py:25
  75.9 8.1 %collective-permute-start.11 = (f32[2,192,128]{2,1,0:T(8,128)S(1)}, f32[2,192,128]{2,1,0:T(8,128)S(1)}, u32[]{:S(2)}, u32[]{:S(2)}) collective-permute-start(f32[2,192,128]{2,1,0:T(8,128)S(1)} %get-tuple-element.31), channel_id=1, source_target_pairs={{0,1},{1,2},{2,3},{4,5},{5,6},{6,7},{8,9},{9,10},{10,11},{12,13},{... | collective-permute-start | bytes 589832 | tf_op jit(solution)/shard_map/ppermute | solution.py:22
  83.6 0.7 copy-start.8
  83.9 0.7 copy-start.10
  87.2 9.2 %collective-permute-start.12 = (f32[2,192,128]{2,1,0:T(8,128)}, f32[2,192,128]{2,1,0:T(8,128)}, u32[]{:S(2)}, u32[]{:S(2)}) collective-permute-start(f32[2,192,128]{2,1,0:T(8,128)} %get-tuple-element.28), channel_id=1, source_target_pairs={{1,0},{2,1},{3,2},{5,4},{6,5},{7,6},{9,8},{10,9},{11,10},{13,12},{... | collective-permute-start | bytes 589832 | tf_op jit(solution)/shard_map/ppermute | solution.py:25
  88.5 8.5 %collective-permute-start.13 = (f32[2,192,128]{2,1,0:T(8,128)}, f32[2,192,128]{2,1,0:T(8,128)}, u32[]{:S(2)}, u32[]{:S(2)}) collective-permute-start(f32[2,192,128]{2,1,0:T(8,128)} %get-tuple-element.29), channel_id=1, source_target_pairs={{0,1},{1,2},{2,3},{4,5},{5,6},{6,7},{8,9},{9,10},{10,11},{12,13},{... | collective-permute-start | bytes 589832 | tf_op jit(solution)/shard_map/ppermute | solution.py:22
  98.9 1.8 %collective-permute-start.14 = (f32[4,192,128]{2,1,0:T(8,128)S(1)}, f32[4,192,128]{2,1,0:T(8,128)S(1)}, u32[]{:S(2)}, u32[]{:S(2)}) collective-permute-start(f32[4,192,128]{2,1,0:T(8,128)S(1)} %fusion.4), channel_id=1, source_target_pairs={{0,4},{4,0},{8,12},{12,8},{1,5},{5,1},{9,13},{13,9},{2,6},{6,2},{1... | collective-permute-start | bytes 1179656 | tf_op jit(solution)/shard_map/ppermute | solution.py:121
  100.7 11.2 %collective-permute-start.15 = (f32[4,192,128]{2,1,0:T(8,128)S(1)}, f32[4,192,128]{2,1,0:T(8,128)S(1)}, u32[]{:S(2)}, u32[]{:S(2)}) collective-permute-start(f32[4,192,128]{2,1,0:T(8,128)S(1)} %add.519), channel_id=1, source_target_pairs={{0,8},{4,12},{8,0},{12,4},{1,9},{5,13},{9,1},{13,5},{2,10},{6,14},... | collective-permute-start | bytes 1179656 | tf_op jit(solution)/shard_map/ppermute | solution.py:121
